TPU v7x, 32 devices: a whole 2x2x4 slice. The times are simulated.
32 devices in a mesh: groups: 2 (over x), seq: 16 (over z, y, core).
Axes of the slice: x: 2, y: 2, z: 4, core: 2. Of those that a mesh axis runs over, the one named last changes fastest.
Arguments:
- tokens: bfloat16 [4096, 1152], P(('groups', 'seq')), parts along dimension 0, may hold values from -30 to 30
- shift_cond: float32 [2304], P('groups'), parts along dimension 0, may hold values from -3 to 3
- scale_cond: float32 [2304], P('groups'), parts along dimension 0, may hold values from -3 to 3
- gate_cond: float32 [2304], P('groups'), parts along dimension 0, may hold values from -4 to 4
- qkv_weight: bfloat16 [1152, 3456], replicated, may hold values from -2 to 2
- out_weight: bfloat16 [1152, 1152], replicated, may hold values from -0.1875 to 0.1875
- cotangent: bfloat16 [4096, 1152], P(('groups', 'seq')), parts along dimension 0, may hold values from -6 to 6
Outputs:
- block_output: bfloat16 [4096, 1152], P(('groups', 'seq')), parts along dimension 0
- grad_input: bfloat16 [4096, 1152], P(('groups', 'seq')), parts along dimension 0
- grad_condition: float32 [6, 1152], P('groups'), parts along dimension 0
There are 2 independent parts, one for each index of `groups`. A program takes and returns all parts, laid end to end along the dimension named above; an argument that names none is the same for every part. Nothing has to cross between parts.
All inputs are finite; a program needn't handle non-finite values.
Results may differ from a plain program's by a relative error of at most 0.012.
The roundings to bfloat16 on the way count: a program that leaves them out, or rounds other values in their place, can miss the bound.
Values may be sent and summed in bfloat16 or wider, within the bound.
No kernel may reach another device: no remote copies, remote signals or barrier semaphores. Data moves between devices by JAX's collectives and lax.ppermute only.
A program may use at most 128 MiB of HBM per device.

v0:
```python
import math
import jax
import jax.numpy as jnp
from jax import lax
from jax.sharding import PartitionSpec as P

H = 16


def from_partner(shard, axis, stride):
    return lax.ppermute(shard, axis, [(i, i ^ 1 << stride) for i in range(lax.axis_size(axis))])


def per_device(tokens, shift_cond, scale_cond, gate_cond, qkv_weight, out_weight, cotangent):
    seq_count = lax.axis_size("seq")
    repeat = seq_count // H
    levels = repeat.bit_length() - 1
    tok_rows = tokens.shape[0]
    model_width = tokens.shape[1]
    head_size = model_width // H
    sub_rows = tok_rows // repeat
    att_scale = 1.0 / math.sqrt(head_size)
    tokens_wide = tokens.astype(jnp.float32)
    row_mean = jnp.mean(tokens_wide, axis=1, keepdims=True)
    centered = tokens_wide - row_mean
    variance = jnp.mean(centered * centered, axis=1, keepdims=True)
    inv_std = lax.rsqrt(variance + 1e-06)
    normed = centered * inv_std
    modulated = (normed * (1.0 + scale_cond) + shift_cond).astype(jnp.bfloat16)
    qkv_cols = lax.dot_general(
        qkv_weight, modulated, (((0,), (1,)), ((), ())), preferred_element_type=jnp.float32
    ).astype(jnp.bfloat16)
    qkv_grid = qkv_cols.reshape(3, H, head_size, repeat, sub_rows).transpose(0, 1, 3, 2, 4)
    qkv_grid = qkv_grid.reshape(3, seq_count, head_size, sub_rows)
    landed = lax.all_to_all(qkv_grid, "seq", split_axis=1, concat_axis=3, tiled=True)
    queries = landed[0, 0]
    key_value = landed[1:, 0]
    for level in range(levels):
        partner = from_partner(key_value, "seq", level)
        key_value = jnp.concatenate([key_value, partner], axis=2)
    key_cols = key_value[0]
    value_cols = key_value[1]
    query_len = queries.shape[1]
    key_len = key_cols.shape[1]
    block_len = math.gcd(512, query_len)
    block_count = query_len // block_len
    query_blocks = queries.reshape(head_size, block_count, block_len).transpose(1, 0, 2)

    def forward_block(query_block):
        scores = (
            lax.dot_general(
                query_block, key_cols, (((0,), (0,)), ((), ())), preferred_element_type=jnp.float32
            )
            * att_scale
        )
        row_max = jnp.max(scores, axis=1, keepdims=True)
        exponent = jnp.exp(scores - row_max)
        weights = (exponent / jnp.sum(exponent, axis=1, keepdims=True)).astype(jnp.bfloat16)
        head_result = lax.dot_general(
            value_cols, weights, (((1,), (1,)), ((), ())), preferred_element_type=jnp.float32
        ).astype(jnp.bfloat16)
        return (weights, head_result)

    weights_all, head_out = lax.map(forward_block, query_blocks)
    attended = head_out.transpose(1, 0, 2).reshape(1, head_size, query_len)
    returned = lax.all_to_all(attended, "seq", split_axis=2, concat_axis=0, tiled=True)
    attended_cols = returned.reshape(H, repeat, head_size, sub_rows).transpose(0, 2, 1, 3)
    attended_cols = attended_cols.reshape(model_width, tok_rows)
    branch = lax.dot_general(
        attended_cols, out_weight, (((0,), (0,)), ((), ())), preferred_element_type=jnp.float32
    )
    block_output = (tokens_wide + gate_cond * branch).astype(jnp.bfloat16)
    cot_wide = cotangent.astype(jnp.float32)
    gated_grad = (gate_cond * cot_wide).astype(jnp.bfloat16)
    gate_grad = jnp.sum(cot_wide * branch, axis=0)
    attended_grad = lax.dot_general(
        out_weight, gated_grad, (((1,), (1,)), ((), ())), preferred_element_type=jnp.float32
    ).astype(jnp.bfloat16)
    grad_grid = attended_grad.reshape(H, head_size, repeat, sub_rows).transpose(0, 2, 1, 3)
    grad_grid = grad_grid.reshape(seq_count, head_size, sub_rows)
    out_grads = lax.all_to_all(grad_grid, "seq", split_axis=0, concat_axis=2, tiled=True)[0]
    grad_blocks = out_grads.reshape(head_size, block_count, block_len).transpose(1, 0, 2)

    def backward_step(total_grad, block_items):
        query_block, out_block, grad_block, weight_block = block_items
        prob_grad = lax.dot_general(
            grad_block, value_cols, (((0,), (0,)), ((), ())), preferred_element_type=jnp.float32
        )
        row_delta = jnp.sum(out_block.astype(jnp.float32) * grad_block.astype(jnp.float32), axis=0)
        score_grad = (
            weight_block.astype(jnp.float32) * (prob_grad - row_delta[:, None]) * att_scale
        ).astype(jnp.bfloat16)
        query_grad = lax.dot_general(
            key_cols, score_grad, (((1,), (1,)), ((), ())), preferred_element_type=jnp.float32
        ).astype(jnp.bfloat16)
        key_grad = lax.dot_general(
            query_block, score_grad, (((1,), (0,)), ((), ())), preferred_element_type=jnp.float32
        )
        value_grad = lax.dot_general(
            grad_block, weight_block, (((1,), (0,)), ((), ())), preferred_element_type=jnp.float32
        )
        return (total_grad + jnp.stack([key_grad, value_grad]), query_grad)

    start_grad = jnp.zeros((2, head_size, key_len), jnp.float32)
    pair_grads, query_grads = lax.scan(
        backward_step, start_grad, (query_blocks, head_out, grad_blocks, weights_all)
    )
    query_grad_all = query_grads.transpose(1, 0, 2).reshape(head_size, query_len)
    for level in reversed(range(levels)):
        middle = pair_grads.shape[2] // 2
        partner = from_partner(pair_grads[:, :, middle:], "seq", level)
        pair_grads = pair_grads[:, :, :middle] + partner
    stacked = jnp.concatenate([query_grad_all[None], pair_grads.astype(jnp.bfloat16)], axis=0)
    came_back = lax.all_to_all(
        stacked.reshape(3, 1, head_size, query_len), "seq", split_axis=3, concat_axis=1, tiled=True
    )
    qkv_grad = came_back.reshape(3, H, repeat, head_size, sub_rows).transpose(0, 1, 3, 2, 4)
    qkv_grad = qkv_grad.reshape(3 * model_width, tok_rows)
    modulated_grad = lax.dot_general(
        qkv_grad, qkv_weight, (((0,), (1,)), ((), ())), preferred_element_type=jnp.float32
    )
    local_sums = jnp.stack(
        [jnp.sum(modulated_grad, axis=0), jnp.sum(modulated_grad * normed, axis=0), gate_grad]
    )
    mod_sums = lax.psum(local_sums, "seq")
    grad_condition = mod_sums / math.sqrt(tok_rows * seq_count)
    normed_grad = modulated_grad * (1.0 + scale_cond)
    first_mean = jnp.mean(normed_grad, axis=1, keepdims=True)
    second_mean = jnp.mean(normed_grad * normed, axis=1, keepdims=True)
    grad_input = (cot_wide + inv_std * (normed_grad - first_mean - normed * second_mean)).astype(
        jnp.bfloat16
    )
    return (block_output, grad_input, grad_condition)


def solution(mesh):
    return jax.shard_map(
        per_device,
        mesh=mesh,
        in_specs=(
            P(("groups", "seq"), None),
            P("groups"),
            P("groups"),
            P("groups"),
            P(),
            P(),
            P(("groups", "seq"), None),
        ),
        out_specs=(P(("groups", "seq"), None), P(("groups", "seq"), None), P("groups", None)),
        check_vma=False,
    )
```

profile of v0, /device:TPU:0, one launch (start us, length us, event | category | flops | bytes accessed | tf_op | source)
XLA Modules:
  0.0 287.5 jit_solution(3109054477897225463)
XLA Ops:
  5.2 7.4 %all-to-all-start.2 = ((bf16[16,72,128]{2,1,0:T(8,128)(2,1)}), bf16[16,72,128]{2,1,0:T(8,128)(2,1)}, u32[]{:S(2)}, u32[]{:S(2)}) async-start(bf16[16,72,128]{2,1,0:T(8,128)(2,1)} %bitcast.14), calls=%async_computation.2 | async-start | bytes 589824 | tf_op jit(solution)/shard_map/all_to_all | solution.py:81
  13.0 5.6 %fusion.21 = bf16[3456,128]{0,1:T(8,128)(2,1)} fusion(bf16[1152,3456]{1,0:T(8,128)(2,1)} %param.15, bf16[128,1152]{1,0:T(8,128)(2,1)S(1)} %copy-done.2, f32[1152]{0:T(1024)S(1)} %copy-done.6, f32[1152]{0:T(1024)S(1)} %broadcast_add_fusion, f32[128]{0:T(128)S(1)} %add_rsqrt_fusion, f32[128]{0:T(128)S(1)} %broadcast_multiply_fusion.3), kind=kOutput, calls=%fused_computation.33 | convolution fusion | flops 1020542976 | bytes 9152512 | tf_op jit(solution)/shard_map/dot_general | solution.py:30
  23.2 4.3 %all-to-all-start = ((bf16[3,16,72,128]{3,2,0,1:T(8,128)(2,1)}), bf16[3,16,72,128]{3,2,0,1:T(8,128)(2,1)S(1)}, u32[]{:S(2)}, u32[]{:S(2)}) async-start(bf16[3,16,72,128]{3,2,0,1:T(8,128)(2,1)} %copy.72), calls=%async_computation | async-start | bytes 1769472 | tf_op jit(solution)/shard_map/all_to_all | solution.py:35
  32.8 15.0 %all-to-all-done = bf16[3,16,72,128]{3,2,0,1:T(8,128)(2,1)S(1)} async-done(((bf16[3,16,72,128]{3,2,0,1:T(8,128)(2,1)}), bf16[3,16,72,128]{3,2,0,1:T(8,128)(2,1)S(1)}, u32[]{:S(2)}, u32[]{:S(2)}) %all-to-all-start) | async-done | bytes 884768 | tf_op jit(solution)/shard_map/all_to_all | solution.py:35
  53.0 28.4 %while.25 = (s32[]{:T(128)}, bf16[4,512,2048]{2,1,0:T(8,128)(2,1)}, bf16[4,72,512]{2,1,0:T(8,128)(2,1)}, bf16[4,72,512]{2,1,0:T(8,128)(2,1)}, bf16[72,2048]{1,0:...) while((s32[]{:T(128)}, bf16[4,512,2048]{2,1,0:T(8,128)(2,1)}, bf16[4,72,512]{2,1,0:T(8,128)(2,1)}, ...), condition=%wide.region_5.6_spmd, body=%wide.region_2.5_spmd.sunk | while | flops 311462912 | bytes 19623500 | solution.py:64
  82.1 59.1 %while.26 = (s32[]{:T(128)}, f32[2,72,2048]{2,1,0:T(8,128)}, bf16[4,72,512]{2,1,0:T(8,128)(2,1)}, bf16[4,72,512]{2,1,0:T(8,128)(2,1)}, bf16[4,512,2048]{2,1,0:T(...) while((s32[]{:T(128)}, f32[2,72,2048]{2,1,0:T(8,128)}, ...), condition=%wide.region_8.9_spmd.clone, body=%wide.region_6.8_spmd.clone.sunk | while | flops 610291200 | bytes 24632472 | solution.py:105
  93.6 3.0 %fusion.90 = bf16[4,72,512]{2,1,0:T(8,128)(2,1)} fusion(bf16[4,72,512]{2,1,0:T(8,128)(2,1)} %get-tuple-element.374, s32[]{:T(128)} %get-tuple-element.372, bf16[512,2048]{1,0:T(8,128)(2,1)} %copy-done.1, bf16[72,2048]{1,0:T(8,128)(2,1)S(1)} %get-tuple-element.391), kind=kOutput, calls=%fused_computation.20.clone.1 | convolution fusion | flops 151031808 | bytes 2466304 | tf_op jit(solution)/shard_map/while/body/eval_jaxpr/dot_general | solution.py:93
  105.8 2.6 maximum_add_fusion.2
  108.4 3.0 %fusion.90 = bf16[4,72,512]{2,1,0:T(8,128)(2,1)} fusion(bf16[4,72,512]{2,1,0:T(8,128)(2,1)} %get-tuple-element.374, s32[]{:T(128)} %get-tuple-element.372, bf16[512,2048]{1,0:T(8,128)(2,1)} %copy-done.1, bf16[72,2048]{1,0:T(8,128)(2,1)S(1)} %get-tuple-element.391), kind=kOutput, calls=%fused_computation.20.clone.1 | convolution fusion | flops 151031808 | bytes 2466304 | tf_op jit(solution)/shard_map/while/body/eval_jaxpr/dot_general | solution.py:93
  120.7 2.6 maximum_add_fusion.2
  123.3 3.0 %fusion.90 = bf16[4,72,512]{2,1,0:T(8,128)(2,1)} fusion(bf16[4,72,512]{2,1,0:T(8,128)(2,1)} %get-tuple-element.374, s32[]{:T(128)} %get-tuple-element.372, bf16[512,2048]{1,0:T(8,128)(2,1)} %copy-done.1, bf16[72,2048]{1,0:T(8,128)(2,1)S(1)} %get-tuple-element.391), kind=kOutput, calls=%fused_computation.20.clone.1 | convolution fusion | flops 151031808 | bytes 2466304 | tf_op jit(solution)/shard_map/while/body/eval_jaxpr/dot_general | solution.py:93
  135.6 2.6 maximum_add_fusion.2
  138.2 3.0 %fusion.90 = bf16[4,72,512]{2,1,0:T(8,128)(2,1)} fusion(bf16[4,72,512]{2,1,0:T(8,128)(2,1)} %get-tuple-element.374, s32[]{:T(128)} %get-tuple-element.372, bf16[512,2048]{1,0:T(8,128)(2,1)} %copy-done.1, bf16[72,2048]{1,0:T(8,128)(2,1)S(1)} %get-tuple-element.391), kind=kOutput, calls=%fused_computation.20.clone.1 | convolution fusion | flops 151031808 | bytes 2466304 | tf_op jit(solution)/shard_map/while/body/eval_jaxpr/dot_general | solution.py:93
  148.8 12.8 %reduce = bf16[2048,72]{1,0:T(8,128)(2,1)S(1)} reduce(bf16[2048,1,72]{2,1,0:T(2,128)(2,1)} %bitcast.144, bf16[]{:T(256)} %broadcast.71), dimensions={1}, to_apply=%bitcast.81.reduce_sub_computation | reduce | bytes 589826
  163.4 6.0 %all-to-all-start.1 = ((bf16[16,2,4608]{2,1,0:T(2,128)(2,1)}), bf16[16,2,4608]{2,1,0:T(2,128)(2,1)}, u32[]{:S(2)}, u32[]{:S(2)}) async-start(bf16[16,2,4608]{2,1,0:T(2,128)(2,1)} %reshape.56), calls=%async_computation.1 | async-start | bytes 589824 | tf_op jit(solution)/shard_map/all_to_all | solution.py:66
  173.2 3.0 %bitcast_bitcast_fusion.1 = bf16[2048,1,3,72]{3,2,1,0:T(4,128)(2,1)} fusion(bf16[3,72,2048]{1,0,2:T(4,128)(2,1)} %copy.86), kind=kLoop, calls=%fused_computation.77 | loop fusion | bytes 1769472
  176.2 5.0 %reshape.58 = bf16[16,2,13824]{2,1,0:T(2,128)(2,1)} reshape(bf16[2048,1,3,72]{3,2,1,0:T(4,128)(2,1)} %bitcast_bitcast_fusion.1) | data formatting | bytes 1769472
  181.2 6.0 %all-to-all-start.3 = ((bf16[16,2,13824]{2,1,0:T(2,128)(2,1)}), bf16[16,2,13824]{2,1,0:T(2,128)(2,1)}, u32[]{:S(2)}, u32[]{:S(2)}) async-start(bf16[16,2,13824]{2,1,0:T(2,128)(2,1)} %reshape.58), calls=%async_computation.3 | async-start | bytes 1769472 | tf_op jit(solution)/shard_map/all_to_all | solution.py:114
  187.2 4.1 %reshape.57 = bf16[2048,1,72]{2,1,0:T(2,128)(2,1)} reshape(bf16[16,2,4608]{2,1,0:T(2,128)(2,1)} %all-to-all-done.1) | data formatting | bytes 589824
  193.8 13.8 %all-to-all-done.3 = bf16[16,2,13824]{2,1,0:T(2,128)(2,1)} async-done(((bf16[16,2,13824]{2,1,0:T(2,128)(2,1)}), bf16[16,2,13824]{2,1,0:T(2,128)(2,1)}, u32[]{:S(2)}, u32[]{:S(2)}) %all-to-all-start.3) | async-done | bytes 884768 | tf_op jit(solution)/shard_map/all_to_all | solution.py:114
  207.6 5.4 %reshape.59 = bf16[2048,1,3,72]{3,2,1,0:T(4,128)(2,1)} reshape(bf16[16,2,13824]{2,1,0:T(2,128)(2,1)} %all-to-all-done.3) | data formatting | bytes 1769472
  213.0 3.9 %copy.91 = bf16[3,1,72,16,128]{4,2,3,0,1:T(8,128)(2,1)} copy(bf16[3,1,72,16,128]{2,0,4,3,1:T(4,128)(2,1)} %bitcast.143) | data formatting | bytes 1769472 | tf_op jit(solution)/shard_map/all_to_all | solution.py:114
  216.9 6.2 %fusion.34 = (f32[1152]{0:T(1024)S(1)}, f32[128]{0:T(128)S(1)}, f32[128]{0:T(128)S(1)}, f32[1152]{0:T(1024)S(1)}, f32[128,1152]{1,0:T(8,128)S(1)}) fusion(bf16[128,1152]{1,0:T(8,128)(2,1)S(1)} %copy-done.3, f32[128]{0:T(128)S(1)} %add_rsqrt_fusion, f32[128]{0:T(128)S(1)} %broadcast_multiply_fusion.3, f32[1152]{0:T(1024)S(1)} %broadcast_add_fusion, ...), kind=kOutput, calls=%fused_computation.54 | convolution fusion | flops 1020687872 | bytes 9747968 | tf_op jit(solution)/shard_map/dot_general | solution.py:119
  224.9 62.0 %psum.7 = f32[3,1152]{1,0:T(4,128)S(1)} all-reduce(f32[3,1152]{1,0:T(4,128)S(1)} %pad_maximum_fusion.1), channel_id=1, replica_groups=mesh['groups'=2,'seq'=16] {'seq'}, use_global_device_ids=true, to_apply=%region_14.15 | all-reduce | flops 3456 | bytes 27648 | tf_op jit(solution)/shard_map/psum | solution.py:125
  (101 shorter events, 106.0 us)
Async XLA Ops:
  0.6 1.8 copy-start
  0.6 12.0 %copy-start.2 = (bf16[128,1152]{1,0:T(8,128)(2,1)S(1)}, bf16[128,1152]{1,0:T(8,128)(2,1)}, u32[]{:S(2)}) copy-start(bf16[128,1152]{1,0:T(8,128)(2,1)} %param.11) | copy-start | bytes 884740
  0.7 12.3 %copy-start.7 = (f32[1152]{0:T(1024)S(1)}, f32[1152]{0:T(1024)}, u32[]{:S(2)}) copy-start(f32[1152]{0:T(1024)} %param.13) | copy-start | bytes 13828
  0.7 12.3 %copy-start.6 = (f32[1152]{0:T(1024)S(1)}, f32[1152]{0:T(1024)}, u32[]{:S(2)}) copy-start(f32[1152]{0:T(1024)} %param.12) | copy-start | bytes 13828
  5.2 18.1 %all-to-all-start.2 = ((bf16[16,72,128]{2,1,0:T(8,128)(2,1)}), bf16[16,72,128]{2,1,0:T(8,128)(2,1)}, u32[]{:S(2)}, u32[]{:S(2)}) async-start(bf16[16,72,128]{2,1,0:T(8,128)(2,1)} %bitcast.14), calls=%async_computation.2 | async-start | bytes 589824 | tf_op jit(solution)/shard_map/all_to_all | solution.py:81
  23.2 24.6 %all-to-all-start = ((bf16[3,16,72,128]{3,2,0,1:T(8,128)(2,1)}), bf16[3,16,72,128]{3,2,0,1:T(8,128)(2,1)S(1)}, u32[]{:S(2)}, u32[]{:S(2)}) async-start(bf16[3,16,72,128]{3,2,0,1:T(8,128)(2,1)} %copy.72), calls=%async_computation | async-start | bytes 1769472 | tf_op jit(solution)/shard_map/all_to_all | solution.py:35
  85.6 1.4 copy-start.1
  100.1 1.4 copy-start.1
  115.0 1.4 copy-start.1
  129.8 1.4 copy-start.1
  163.4 17.8 %all-to-all-start.1 = ((bf16[16,2,4608]{2,1,0:T(2,128)(2,1)}), bf16[16,2,4608]{2,1,0:T(2,128)(2,1)}, u32[]{:S(2)}, u32[]{:S(2)}) async-start(bf16[16,2,4608]{2,1,0:T(2,128)(2,1)} %reshape.56), calls=%async_computation.1 | async-start | bytes 589824 | tf_op jit(solution)/shard_map/all_to_all | solution.py:66
  181.2 26.4 %all-to-all-start.3 = ((bf16[16,2,13824]{2,1,0:T(2,128)(2,1)}), bf16[16,2,13824]{2,1,0:T(2,128)(2,1)}, u32[]{:S(2)}, u32[]{:S(2)}) async-start(bf16[16,2,13824]{2,1,0:T(2,128)(2,1)} %reshape.58), calls=%async_computation.3 | async-start | bytes 1769472 | tf_op jit(solution)/shard_map/all_to_all | solution.py:114
  193.6 23.3 %copy-start.3 = (bf16[128,1152]{1,0:T(8,128)(2,1)S(1)}, bf16[128,1152]{1,0:T(8,128)(2,1)}, u32[]{:S(2)}) copy-start(bf16[128,1152]{1,0:T(8,128)(2,1)} %param.11) | copy-start | bytes 884740
  216.9 6.3 %copy-start.4 = (bf16[128,1152]{1,0:T(8,128)(2,1)S(1)}, bf16[128,1152]{1,0:T(8,128)(2,1)}, u32[]{:S(2)}) copy-start(bf16[128,1152]{1,0:T(8,128)(2,1)} %param.17) | copy-start | bytes 884740
  216.9 6.3 %copy-start.5 = (f32[1152]{0:T(1024)S(1)}, f32[1152]{0:T(1024)}, u32[]{:S(2)}) copy-start(f32[1152]{0:T(1024)} %param.14) | copy-start | bytes 13828
where the time goes:
time: 290 us; the launch traced here: 288 us
  matrix products  71.2 us (25%)
  blocking collectives  62 us (21%)
  local copies, waits for them, and re-layouts  55.9 us (19%)
  other arithmetic  43.2 us (15%)
  waiting for transfers between devices  30.4 us (10%)
  starting transfers between devices  23.8 us (8%)
    psum x1, blocking collectives, per_device(): mod_sums = lax.psum(local_sums, 'seq')  62 us
    unnamed x22, local copies, waits for them, and re-layouts  23.4 us
    all_to_all x1, waiting for transfers between devices, per_device(): lax.all_to_all(qkv_grid, 'seq', split_axis=1, concat_axis=3, tiled=True)  15 us
    all_to_all x1, waiting for transfers between devices, per_device(): lax.all_to_all(stacked.reshape(3, 1, head_size, query_len), 'seq', split_...  13.8 us
    unnamed x2, other arithmetic  12.8 us
    dot_general x4, matrix products, backward_step(): lax.dot_general(key_cols, score_grad, (((1,), (1,)), ((), ())), preferred...  12 us
    dot_general x4, matrix products, backward_step(): lax.dot_general(grad_block, value_cols, (((0,), (0,)), ((), ())), preferr...  10.3 us
    add x4, other arithmetic, backward_step(): return (total_grad + jnp.stack([key_grad, value_grad]), query_grad)  10.1 us
  transfers between devices with their start and end apart: 4, of which 3 were waited for; matrix products, arithmetic and copies ran while one was open for 11% of the time, Pallas kernels for 0%

commit v1 on v0

--- a/solution.py
+++ b/solution.py
@@ -122,7 +122,7 @@
     local_sums = jnp.stack(
         [jnp.sum(modulated_grad, axis=0), jnp.sum(modulated_grad * normed, axis=0), gate_grad]
     )
-    mod_sums = lax.psum(local_sums, "seq")
+    mod_sums = jnp.sum(lax.all_gather(local_sums, "seq"), axis=0)
     grad_condition = mod_sums / math.sqrt(tok_rows * seq_count)
     normed_grad = modulated_grad * (1.0 + scale_cond)
     first_mean = jnp.mean(normed_grad, axis=1, keepdims=True)

time: 290 us -> 251 us (0.87)
  blocking collectives: 62 us -> 22.5 us
    psum x1 -> x0, blocking collectives: 62 us -> none  [per_device(): mod_sums = lax.psum(local_sums, 'seq')]
    all_gather x0 -> x1, blocking collectives: none -> 22.5 us  [per_device(): mod_sums = jnp.sum(lax.all_gather(local_sums, 'seq'), axis=0)]
    unnamed x2 -> x3, other arithmetic: 12.8 us -> 12.8 us
  transfers between devices with their start and end apart: 4 -> 4, of which waited for: 3 -> 3; matrix products, arithmetic and copies ran while one was open for 11% -> 13% of each run, Pallas kernels for 0% -> 0%
where the time goes in v1:
time: 251 us; the launch traced here: 248 us
  matrix products  71.2 us (28%)
  local copies, waits for them, and re-layouts  55.9 us (22%)
  other arithmetic  43.3 us (17%)
  waiting for transfers between devices  30.4 us (12%)
  starting transfers between devices  23.8 us (9%)
  blocking collectives  22.5 us (9%)
    unnamed x22, local copies, waits for them, and re-layouts  23.4 us
    all_gather x1, blocking collectives, per_device(): mod_sums = jnp.sum(lax.all_gather(local_sums, 'seq'), axis=0)  22.5 us
    all_to_all x1, waiting for transfers between devices, per_device(): lax.all_to_all(qkv_grid, 'seq', split_axis=1, concat_axis=3, tiled=True)  15 us
    all_to_all x1, waiting for transfers between devices, per_device(): lax.all_to_all(stacked.reshape(3, 1, head_size, query_len), 'seq', split_...  13.8 us
    unnamed x3, other arithmetic  12.8 us
    dot_general x4, matrix products, backward_step(): lax.dot_general(key_cols, score_grad, (((1,), (1,)), ((), ())), preferred...  12 us
    dot_general x4, matrix products, backward_step(): lax.dot_general(grad_block, value_cols, (((0,), (0,)), ((), ())), preferr...  10.3 us
    add x4, other arithmetic, backward_step(): return (total_grad + jnp.stack([key_grad, value_grad]), query_grad)  10.1 us
  transfers between devices with their start and end apart: 4, of which 3 were waited for; matrix products, arithmetic and copies ran while one was open for 13% of the time, Pallas kernels for 0%

profile of v1, /device:TPU:0, one launch (start us, length us, event | category | flops | bytes accessed | tf_op | source)
XLA Modules:
  0.0 248.1 jit_solution(12070527877069143583)
XLA Ops:
  5.2 7.4 %all-to-all-start.2 = ((bf16[16,72,128]{2,1,0:T(8,128)(2,1)}), bf16[16,72,128]{2,1,0:T(8,128)(2,1)}, u32[]{:S(2)}, u32[]{:S(2)}) async-start(bf16[16,72,128]{2,1,0:T(8,128)(2,1)} %bitcast.14), calls=%async_computation.2 | async-start | bytes 589824 | tf_op jit(solution)/shard_map/all_to_all | solution.py:81
  13.0 5.6 %fusion.21 = bf16[3456,128]{0,1:T(8,128)(2,1)} fusion(bf16[1152,3456]{1,0:T(8,128)(2,1)} %param.15, bf16[128,1152]{1,0:T(8,128)(2,1)S(1)} %copy-done.2, f32[1152]{0:T(1024)S(1)} %copy-done.6, f32[1152]{0:T(1024)S(1)} %broadcast_add_fusion, f32[128]{0:T(128)S(1)} %add_rsqrt_fusion, f32[128]{0:T(128)S(1)} %broadcast_multiply_fusion.3), kind=kOutput, calls=%fused_computation.33 | convolution fusion | flops 1020542976 | bytes 9152512 | tf_op jit(solution)/shard_map/dot_general | solution.py:30
  23.2 4.3 %all-to-all-start = ((bf16[3,16,72,128]{3,2,0,1:T(8,128)(2,1)}), bf16[3,16,72,128]{3,2,0,1:T(8,128)(2,1)S(1)}, u32[]{:S(2)}, u32[]{:S(2)}) async-start(bf16[3,16,72,128]{3,2,0,1:T(8,128)(2,1)} %copy.72), calls=%async_computation | async-start | bytes 1769472 | tf_op jit(solution)/shard_map/all_to_all | solution.py:35
  32.8 15.0 %all-to-all-done = bf16[3,16,72,128]{3,2,0,1:T(8,128)(2,1)S(1)} async-done(((bf16[3,16,72,128]{3,2,0,1:T(8,128)(2,1)}), bf16[3,16,72,128]{3,2,0,1:T(8,128)(2,1)S(1)}, u32[]{:S(2)}, u32[]{:S(2)}) %all-to-all-start) | async-done | bytes 884768 | tf_op jit(solution)/shard_map/all_to_all | solution.py:35
  53.0 28.4 %while.25 = (s32[]{:T(128)}, bf16[4,512,2048]{2,1,0:T(8,128)(2,1)}, bf16[4,72,512]{2,1,0:T(8,128)(2,1)}, bf16[4,72,512]{2,1,0:T(8,128)(2,1)}, bf16[72,2048]{1,0:...) while((s32[]{:T(128)}, bf16[4,512,2048]{2,1,0:T(8,128)(2,1)}, bf16[4,72,512]{2,1,0:T(8,128)(2,1)}, ...), condition=%wide.region_5.6_spmd, body=%wide.region_2.5_spmd.sunk | while | flops 311462912 | bytes 19623500 | solution.py:64
  82.1 59.1 %while.26 = (s32[]{:T(128)}, f32[2,72,2048]{2,1,0:T(8,128)}, bf16[4,72,512]{2,1,0:T(8,128)(2,1)}, bf16[4,72,512]{2,1,0:T(8,128)(2,1)}, bf16[4,512,2048]{2,1,0:T(...) while((s32[]{:T(128)}, f32[2,72,2048]{2,1,0:T(8,128)}, ...), condition=%wide.region_8.9_spmd.clone, body=%wide.region_6.8_spmd.clone.sunk | while | flops 610291200 | bytes 24632472 | solution.py:105
  93.6 3.0 %fusion.90 = bf16[4,72,512]{2,1,0:T(8,128)(2,1)} fusion(bf16[4,72,512]{2,1,0:T(8,128)(2,1)} %get-tuple-element.374, s32[]{:T(128)} %get-tuple-element.372, bf16[512,2048]{1,0:T(8,128)(2,1)} %copy-done.1, bf16[72,2048]{1,0:T(8,128)(2,1)S(1)} %get-tuple-element.391), kind=kOutput, calls=%fused_computation.20.clone.1 | convolution fusion | flops 151031808 | bytes 2466304 | tf_op jit(solution)/shard_map/while/body/eval_jaxpr/dot_general | solution.py:93
  105.8 2.6 %maximum_add_fusion.2 = f32[2,72,2048]{2,1,0:T(8,128)} fusion(f32[1,72,2048]{2,1,0:T(8,128)S(1)} %convolution_bitcast_fusion.4, f32[1,72,2048]{2,1,0:T(8,128)} %convolution_bitcast_fusion.5, f32[2,72,2048]{2,1,0:T(8,128)} %get-tuple-element.373, pred[]{:T(512)S(6)} %compare.3), kind=kLoop, calls=%fused_computation.17.clone.1 | loop fusion | flops 884736 | bytes 3538945 | tf_op jit(solution)/shard_map/while/body/eval_jaxpr/add | solution.py:102
  108.4 3.0 %fusion.90 = bf16[4,72,512]{2,1,0:T(8,128)(2,1)} fusion(bf16[4,72,512]{2,1,0:T(8,128)(2,1)} %get-tuple-element.374, s32[]{:T(128)} %get-tuple-element.372, bf16[512,2048]{1,0:T(8,128)(2,1)} %copy-done.1, bf16[72,2048]{1,0:T(8,128)(2,1)S(1)} %get-tuple-element.391), kind=kOutput, calls=%fused_computation.20.clone.1 | convolution fusion | flops 151031808 | bytes 2466304 | tf_op jit(solution)/shard_map/while/body/eval_jaxpr/dot_general | solution.py:93
  120.7 2.6 %maximum_add_fusion.2 = f32[2,72,2048]{2,1,0:T(8,128)} fusion(f32[1,72,2048]{2,1,0:T(8,128)S(1)} %convolution_bitcast_fusion.4, f32[1,72,2048]{2,1,0:T(8,128)} %convolution_bitcast_fusion.5, f32[2,72,2048]{2,1,0:T(8,128)} %get-tuple-element.373, pred[]{:T(512)S(6)} %compare.3), kind=kLoop, calls=%fused_computation.17.clone.1 | loop fusion | flops 884736 | bytes 3538945 | tf_op jit(solution)/shard_map/while/body/eval_jaxpr/add | solution.py:102
  123.3 3.0 %fusion.90 = bf16[4,72,512]{2,1,0:T(8,128)(2,1)} fusion(bf16[4,72,512]{2,1,0:T(8,128)(2,1)} %get-tuple-element.374, s32[]{:T(128)} %get-tuple-element.372, bf16[512,2048]{1,0:T(8,128)(2,1)} %copy-done.1, bf16[72,2048]{1,0:T(8,128)(2,1)S(1)} %get-tuple-element.391), kind=kOutput, calls=%fused_computation.20.clone.1 | convolution fusion | flops 151031808 | bytes 2466304 | tf_op jit(solution)/shard_map/while/body/eval_jaxpr/dot_general | solution.py:93
  135.6 2.6 %maximum_add_fusion.2 = f32[2,72,2048]{2,1,0:T(8,128)} fusion(f32[1,72,2048]{2,1,0:T(8,128)S(1)} %convolution_bitcast_fusion.4, f32[1,72,2048]{2,1,0:T(8,128)} %convolution_bitcast_fusion.5, f32[2,72,2048]{2,1,0:T(8,128)} %get-tuple-element.373, pred[]{:T(512)S(6)} %compare.3), kind=kLoop, calls=%fused_computation.17.clone.1 | loop fusion | flops 884736 | bytes 3538945 | tf_op jit(solution)/shard_map/while/body/eval_jaxpr/add | solution.py:102
  138.2 3.0 %fusion.90 = bf16[4,72,512]{2,1,0:T(8,128)(2,1)} fusion(bf16[4,72,512]{2,1,0:T(8,128)(2,1)} %get-tuple-element.374, s32[]{:T(128)} %get-tuple-element.372, bf16[512,2048]{1,0:T(8,128)(2,1)} %copy-done.1, bf16[72,2048]{1,0:T(8,128)(2,1)S(1)} %get-tuple-element.391), kind=kOutput, calls=%fused_computation.20.clone.1 | convolution fusion | flops 151031808 | bytes 2466304 | tf_op jit(solution)/shard_map/while/body/eval_jaxpr/dot_general | solution.py:93
  148.8 12.8 %reduce.1 = bf16[2048,72]{1,0:T(8,128)(2,1)S(1)} reduce(bf16[2048,1,72]{2,1,0:T(2,128)(2,1)} %bitcast.146, bf16[]{:T(256)} %broadcast.71), dimensions={1}, to_apply=%bitcast.83.reduce_sub_computation | reduce | bytes 589826
  163.4 6.0 %all-to-all-start.1 = ((bf16[16,2,4608]{2,1,0:T(2,128)(2,1)}), bf16[16,2,4608]{2,1,0:T(2,128)(2,1)}, u32[]{:S(2)}, u32[]{:S(2)}) async-start(bf16[16,2,4608]{2,1,0:T(2,128)(2,1)} %reshape.60), calls=%async_computation.1 | async-start | bytes 589824 | tf_op jit(solution)/shard_map/all_to_all | solution.py:66
  173.2 3.0 %bitcast_bitcast_fusion.1 = bf16[2048,1,3,72]{3,2,1,0:T(4,128)(2,1)} fusion(bf16[3,72,2048]{1,0,2:T(4,128)(2,1)} %copy.86), kind=kLoop, calls=%fused_computation.77 | loop fusion | bytes 1769472
  176.2 5.0 %reshape.62 = bf16[16,2,13824]{2,1,0:T(2,128)(2,1)} reshape(bf16[2048,1,3,72]{3,2,1,0:T(4,128)(2,1)} %bitcast_bitcast_fusion.1) | data formatting | bytes 1769472
  181.2 6.0 %all-to-all-start.3 = ((bf16[16,2,13824]{2,1,0:T(2,128)(2,1)}), bf16[16,2,13824]{2,1,0:T(2,128)(2,1)}, u32[]{:S(2)}, u32[]{:S(2)}) async-start(bf16[16,2,13824]{2,1,0:T(2,128)(2,1)} %reshape.62), calls=%async_computation.3 | async-start | bytes 1769472 | tf_op jit(solution)/shard_map/all_to_all | solution.py:114
  187.2 4.1 %reshape.61 = bf16[2048,1,72]{2,1,0:T(2,128)(2,1)} reshape(bf16[16,2,4608]{2,1,0:T(2,128)(2,1)} %all-to-all-done.1) | data formatting | bytes 589824
  193.8 13.8 %all-to-all-done.3 = bf16[16,2,13824]{2,1,0:T(2,128)(2,1)} async-done(((bf16[16,2,13824]{2,1,0:T(2,128)(2,1)}), bf16[16,2,13824]{2,1,0:T(2,128)(2,1)}, u32[]{:S(2)}, u32[]{:S(2)}) %all-to-all-start.3) | async-done | bytes 884768 | tf_op jit(solution)/shard_map/all_to_all | solution.py:114
  207.6 5.4 %reshape.63 = bf16[2048,1,3,72]{3,2,1,0:T(4,128)(2,1)} reshape(bf16[16,2,13824]{2,1,0:T(2,128)(2,1)} %all-to-all-done.3) | data formatting | bytes 1769472
  213.0 3.9 %copy.91 = bf16[3,1,72,16,128]{4,2,3,0,1:T(8,128)(2,1)} copy(bf16[3,1,72,16,128]{2,0,4,3,1:T(4,128)(2,1)} %bitcast.145) | data formatting | bytes 1769472 | tf_op jit(solution)/shard_map/all_to_all | solution.py:114
  216.9 6.2 %fusion.34 = (f32[1152]{0:T(1024)S(1)}, f32[128]{0:T(128)S(1)}, f32[128]{0:T(128)S(1)}, f32[1152]{0:T(1024)S(1)}, f32[128,1152]{1,0:T(8,128)S(1)}) fusion(bf16[128,1152]{1,0:T(8,128)(2,1)S(1)} %copy-done.3, f32[128]{0:T(128)S(1)} %add_rsqrt_fusion, f32[128]{0:T(128)S(1)} %broadcast_multiply_fusion.3, f32[1152]{0:T(1024)S(1)} %broadcast_add_fusion, ...), kind=kOutput, calls=%fused_computation.54 | convolution fusion | flops 1020687872 | bytes 9747968 | tf_op jit(solution)/shard_map/dot_general | solution.py:119
  224.9 22.5 %all-gather.1 = f32[16,3,1152]{2,1,0:T(4,128)S(1)} all-gather(f32[1,3,1152]{2,1,0:T(4,128)S(1)} %maximum_bitcast_fusion), channel_id=2, replica_groups=mesh['groups'=2,'seq'=16] {'seq'}, dimensions={0}, use_global_device_ids=true | all-gather | bytes 235008 | tf_op jit(solution)/shard_map/all_gather | solution.py:125
  (102 shorter events, 106.0 us)
Async XLA Ops:
  0.6 1.8 copy-start
  0.6 12.0 %copy-start.2 = (bf16[128,1152]{1,0:T(8,128)(2,1)S(1)}, bf16[128,1152]{1,0:T(8,128)(2,1)}, u32[]{:S(2)}) copy-start(bf16[128,1152]{1,0:T(8,128)(2,1)} %param.11) | copy-start | bytes 884740
  0.7 12.3 %copy-start.7 = (f32[1152]{0:T(1024)S(1)}, f32[1152]{0:T(1024)}, u32[]{:S(2)}) copy-start(f32[1152]{0:T(1024)} %param.13) | copy-start | bytes 13828
  0.7 12.3 %copy-start.6 = (f32[1152]{0:T(1024)S(1)}, f32[1152]{0:T(1024)}, u32[]{:S(2)}) copy-start(f32[1152]{0:T(1024)} %param.12) | copy-start | bytes 13828
  5.2 18.1 %all-to-all-start.2 = ((bf16[16,72,128]{2,1,0:T(8,128)(2,1)}), bf16[16,72,128]{2,1,0:T(8,128)(2,1)}, u32[]{:S(2)}, u32[]{:S(2)}) async-start(bf16[16,72,128]{2,1,0:T(8,128)(2,1)} %bitcast.14), calls=%async_computation.2 | async-start | bytes 589824 | tf_op jit(solution)/shard_map/all_to_all | solution.py:81
  23.2 24.6 %all-to-all-start = ((bf16[3,16,72,128]{3,2,0,1:T(8,128)(2,1)}), bf16[3,16,72,128]{3,2,0,1:T(8,128)(2,1)S(1)}, u32[]{:S(2)}, u32[]{:S(2)}) async-start(bf16[3,16,72,128]{3,2,0,1:T(8,128)(2,1)} %copy.72), calls=%async_computation | async-start | bytes 1769472 | tf_op jit(solution)/shard_map/all_to_all | solution.py:35
  85.6 1.4 copy-start.1
  100.1 1.4 copy-start.1
  115.0 1.4 copy-start.1
  129.8 1.4 copy-start.1
  163.4 17.8 %all-to-all-start.1 = ((bf16[16,2,4608]{2,1,0:T(2,128)(2,1)}), bf16[16,2,4608]{2,1,0:T(2,128)(2,1)}, u32[]{:S(2)}, u32[]{:S(2)}) async-start(bf16[16,2,4608]{2,1,0:T(2,128)(2,1)} %reshape.60), calls=%async_computation.1 | async-start | bytes 589824 | tf_op jit(solution)/shard_map/all_to_all | solution.py:66
  181.2 26.4 %all-to-all-start.3 = ((bf16[16,2,13824]{2,1,0:T(2,128)(2,1)}), bf16[16,2,13824]{2,1,0:T(2,128)(2,1)}, u32[]{:S(2)}, u32[]{:S(2)}) async-start(bf16[16,2,13824]{2,1,0:T(2,128)(2,1)} %reshape.62), calls=%async_computation.3 | async-start | bytes 1769472 | tf_op jit(solution)/shard_map/all_to_all | solution.py:114
  193.6 23.3 %copy-start.3 = (bf16[128,1152]{1,0:T(8,128)(2,1)S(1)}, bf16[128,1152]{1,0:T(8,128)(2,1)}, u32[]{:S(2)}) copy-start(bf16[128,1152]{1,0:T(8,128)(2,1)} %param.11) | copy-start | bytes 884740
  216.9 6.3 %copy-start.4 = (bf16[128,1152]{1,0:T(8,128)(2,1)S(1)}, bf16[128,1152]{1,0:T(8,128)(2,1)}, u32[]{:S(2)}) copy-start(bf16[128,1152]{1,0:T(8,128)(2,1)} %param.17) | copy-start | bytes 884740
  216.9 6.3 %copy-start.5 = (f32[1152]{0:T(1024)S(1)}, f32[1152]{0:T(1024)}, u32[]{:S(2)}) copy-start(f32[1152]{0:T(1024)} %param.14) | copy-start | bytes 13828
